TPU v7x, 256 devices: a whole 4x4x8 slice. The times are simulated.
256 devices in a mesh: tm: 32 (over z, x), region: 8 (over y, core).
Axes of the slice: x: 4, y: 4, z: 8, core: 2. Of those that a mesh axis runs over, the one named last changes fastest.
Arguments:
- start_primal: float32 [2048, 8, 3200], P('tm', 'region'), may hold values from 0 to 10, as said below
- demand: float32 [2048, 8, 3200], P('tm', 'region'), may hold values from -30 to 30
- unit_cost: float32 [8, 3200], P('region'), may hold values from -5 to 5
- build_cost: float32 [8, 128], P('region', 'tm'), may hold values from 0.5 to 2
- start_capacity: float32 [8, 128], P('region', 'tm'), may hold values from 0 to 2
- net_weights: float32 [8, 25, 3, 128, 128], P('region'), may hold values from -0.3125 to 0.3125
- net_columns: int32 [8, 25, 3], P('region'), may hold values from 0 to 24
- line_weights: float32 [8, 4, 128, 128], P('region'), may hold values from -0.25 to 0.25
- line_source: int32 [8, 4], replicated, may hold values from 0 to 7
- generator_map: int32 [8, 128], P('region'), may hold values from 0 to 127
Outputs:
- primal_final: float32 [2048, 8, 3200], P('tm', 'region')
- dual_final: float32 [2048, 8, 3200], P('tm', 'region')
- capacity_final: float32 [8, 128], P('region', 'tm')
Inputs may be any that keep to these rules, and one draw needn't show every extreme that they name: `start_primal`: Nonnegative.
All inputs are finite; a program needn't handle non-finite values.
Results may differ from a plain program's by a relative error of at most 0.0003.
Values sent between devices are 32-bit elements; how exact they have to be, the bound alone decides.
A program may use at most 64 MiB of HBM per device.

v0:
```python
import math
import jax
import jax.numpy as jnp
from jax import lax
from jax.sharding import PartitionSpec as P

ITERS = 4
HIGHEST_PRECISION = lax.Precision.HIGHEST
STEP_SCALE = 0.2
EPSILON = 1e-06


def shifted(shard, axis, by):
    devices = lax.axis_size(axis)
    pairs = [(i, i + by) for i in range(devices) if 0 <= i + by < devices]
    return lax.ppermute(shard, axis, pairs)


def network_forward(blocks, weights, columns):
    hour_count = blocks.shape[0]
    picked = jnp.take(blocks, columns.reshape(-1), axis=1)
    flat_weights = weights.reshape(-1, weights.shape[2], weights.shape[3])
    product = jnp.einsum("hpk,pkl->hpl", picked, flat_weights, precision=HIGHEST_PRECISION)
    return product.reshape(hour_count, columns.shape[0], columns.shape[1], -1).sum(axis=2)


def network_adjoint(dual_rows, weights, columns):
    hour_count = dual_rows.shape[0]
    partial_value = jnp.einsum("hil,iskl->hisk", dual_rows, weights, precision=HIGHEST_PRECISION)
    block_count = columns.shape[0]
    placing = (columns.reshape(-1)[:, None] == jnp.arange(block_count)[None, :]).astype(jnp.float32)
    stacked = partial_value.reshape(hour_count, -1, partial_value.shape[3])
    return jnp.einsum("hpk,pc->hck", stacked, placing, precision=HIGHEST_PRECISION)


def body(
    start_primal,
    demand,
    unit_cost,
    build_cost,
    start_capacity,
    net_weights,
    net_columns,
    line_weights,
    line_source,
    generator_map,
):
    hour_count, _, row_width = start_primal.shape
    block_size = net_weights.shape[3]
    block_count = row_width // block_size
    tm_count = lax.axis_size("tm")
    region_count = lax.axis_size("region")
    own_region = lax.axis_index("region")
    weights = net_weights[0]
    columns = net_columns[0]
    line_mats = line_weights[0]
    unit_rows = unit_cost.reshape(block_count, block_size)
    invest_own = start_capacity.shape[1]
    invest_all = invest_own * tm_count
    couple = 1.0 / math.sqrt(hour_count * tm_count)
    primal_count = hour_count * tm_count * region_count * row_width + region_count * invest_all
    dual_count = hour_count * tm_count * region_count * row_width
    selector = (generator_map[0][:, None] == jnp.arange(invest_all)[None, :]).astype(jnp.float32)
    line_links = (line_source[:, :, None] == jnp.arange(region_count)[None, None, :]).astype(
        jnp.float32
    )
    own_sources = lax.dynamic_index_in_dim(line_links, own_region, 0, keepdims=False)
    free_column = (jnp.arange(block_count) == 3)[None, :, None]
    free_row = (jnp.arange(block_count) < 3)[None, :, None]
    primal = start_primal.reshape(hour_count, block_count, block_size)
    target = demand.reshape(hour_count, block_count, block_size)
    dual = jnp.zeros_like(primal)
    primal_weight = jnp.float32(1.0)
    capacity, build_rows = (
        lax.all_gather(start_capacity[0], "tm", axis=0, tiled=True),
        lax.all_gather(build_cost[0], "tm", axis=0, tiled=True),
    )
    for iteration in range(ITERS):
        primal_step = STEP_SCALE / primal_weight
        dual_step = STEP_SCALE * primal_weight
        adjoint = network_adjoint(dual, weights, columns)
        after = shifted(dual[0, 0], "tm", -1)
        following = jnp.concatenate([dual[1:, 0], after[None]], axis=0)
        partial_lines = jnp.einsum(
            "hl,jkl->jhk", dual[:, 1], line_mats, precision=HIGHEST_PRECISION
        )
        line_back = lax.psum_scatter(
            jnp.einsum("jq,jhk->qhk", own_sources, partial_lines, precision=HIGHEST_PRECISION),
            "region",
            scatter_dimension=0,
            tiled=True,
        )[0]
        adjoint = adjoint.at[:, 0].add(-following).at[:, 3].add(line_back)
        column_sums = jnp.sum(dual[:, 2], axis=0)
        capacity_part = couple * jnp.dot(column_sums, selector, precision=HIGHEST_PRECISION)
        moved = primal - primal_step * (unit_rows[None] - adjoint)
        new_primal = jnp.where(free_column, moved, jnp.maximum(moved, 0.0))
        capacity_grad = lax.psum(capacity_part, "tm")
        new_capacity = jnp.maximum(capacity - primal_step * (build_rows - capacity_grad), 0.0)
        capacity_bar = 2.0 * new_capacity - capacity
        capacity_change = lax.dynamic_slice_in_dim(
            new_capacity - capacity, lax.axis_index("tm") * invest_own, invest_own, 0
        )
        primal_bar = 2.0 * new_primal - primal
        primal_local = jnp.sum((new_primal - primal) ** 2) + jnp.sum(capacity_change**2)
        if iteration + 1 < ITERS:
            primal_total = lax.psum(primal_local, ("tm", "region"))
        applied = network_forward(primal_bar, weights, columns)
        before = shifted(primal_bar[-1, 0], "tm", 1)
        earlier = jnp.concatenate([before[None], primal_bar[:-1, 0]], axis=0)
        chosen_flows = jnp.einsum(
            "jr,rhk->jhk",
            own_sources,
            lax.all_gather(primal_bar[:, 3][None], "region", axis=0, tiled=True),
            precision=HIGHEST_PRECISION,
        )
        line_flow = jnp.einsum("jhk,jkl->hl", chosen_flows, line_mats, precision=HIGHEST_PRECISION)
        picked_capacity = jnp.dot(selector, capacity_bar, precision=HIGHEST_PRECISION)
        applied = (
            applied.at[:, 0]
            .add(-earlier)
            .at[:, 1]
            .add(line_flow)
            .at[:, 2]
            .add(couple * picked_capacity[None])
        )
        moved_dual = dual + dual_step * (target - applied)
        new_dual = jnp.where(free_row, moved_dual, jnp.maximum(moved_dual, 0.0))
        if iteration + 1 < ITERS:
            dual_local = jnp.sum((new_dual - dual) ** 2)
            dual_total = lax.psum(dual_local, ("tm", "region"))
            primal_weight = jnp.sqrt(
                primal_weight
                * jnp.sqrt(primal_total / primal_count + EPSILON)
                / jnp.sqrt(dual_total / dual_count + EPSILON)
            )
        primal, dual, capacity = (new_primal, new_dual, new_capacity)
    capacity_own = lax.dynamic_slice_in_dim(
        capacity, lax.axis_index("tm") * invest_own, invest_own, 0
    )
    return (
        primal.reshape(hour_count, 1, row_width),
        dual.reshape(hour_count, 1, row_width),
        capacity_own[None],
    )


def solution(mesh):
    in_specs = (
        P("tm", "region", None),
        P("tm", "region", None),
        P("region", None),
        P("region", "tm"),
        P("region", "tm"),
        P("region", None, None, None, None),
        P("region", None, None),
        P("region", None, None, None),
        P(),
        P("region", None),
    )
    out_specs = (P("tm", "region", None), P("tm", "region", None), P("region", "tm"))
    return jax.shard_map(body, mesh=mesh, in_specs=in_specs, out_specs=out_specs, check_vma=False)
```

profile of v0, /device:TPU:1, one launch (start us, length us, event | category | flops | bytes accessed | tf_op | source)
XLA Modules:
  0.0 858.2 jit_solution(13189949462657411320)
XLA Ops:
  12.9 9.0 %fusion.6 = f32[25,64,3,128]{3,1,2,0:T(8,128)S(1)} fusion(f32[1,25,3,128,128]{4,3,2,1,0:T(8,128)} %param.57), kind=kOutput, calls=%fused_computation.10 | convolution fusion | flops 943718400 | bytes 7372800 | tf_op jit(solution)/shard_map/hil,iskl->hisk/dot_general | solution.py:29
  27.1 76.9 %all-reduce.6 = (f32[128]{0:T(128)S(1)}, f32[128]{0:T(128)S(1)}, f32[128]{0:T(128)S(1)}) all-reduce(f32[128]{0:T(128)S(1)} %bitcast_dynamic-update-slice_fusion.1, f32[128]{0:T(128)S(1)} %bitcast_dynamic-update-slice_fusion, f32[128]{0:T(128)S(1)} %fusion.51), channel_id=2, replica_groups=mesh['tm'=32,'region'=8] {'tm'}, use_global_device_ids=true, to_apply=%add.1 | all-reduce | flops 384 | bytes 3072 | tf_op jit(solution)/shard_map/all_gather | solution.py:75
  113.3 28.2 %all-gather.2 = f32[512,1,128]{2,1,0:T(1,128)S(1)} all-gather(f32[64,1,128]{2,1,0:T(1,128)S(1)} %bitcast.385), channel_id=4, replica_groups=mesh['tm'=32,'region'=8] {'region'}, dimensions={0}, use_global_device_ids=true | all-gather | bytes 294912 | tf_op jit(solution)/shard_map/all_gather | solution.py:114
  143.6 7.9 fusion.22
  157.0 10.5 %fusion.4 = f32[25,64,3,128]{3,1,2,0:T(8,128)} fusion(f32[1,25,3,128,128]{4,3,2,1,0:T(8,128)} %param.57, f32[64,25,128]{2,0,1:T(8,128)S(1)} %get-tuple-element.281), kind=kOutput, calls=%fused_computation.8 | convolution fusion | flops 943718400 | bytes 8192000 | tf_op jit(solution)/shard_map/hil,iskl->hisk/dot_general | solution.py:29
  167.7 55.8 %psum.73 = f32[128]{0:T(128)S(1)} all-reduce(f32[128]{0:T(128)S(1)} %fusion.49), channel_id=1, replica_groups=mesh['tm'=32,'region'=8] {'tm'}, use_global_device_ids=true, to_apply=%region_11.13 | all-reduce | flops 128 | bytes 1024 | tf_op jit(solution)/shard_map/psum | solution.py:98
  223.5 89.7 %all-reduce.5 = (f32[]{:T(128)}, f32[]{:T(128)}) all-reduce(f32[]{:T(128)S(6)} %add.249, f32[]{:T(128)} %get-tuple-element.280), channel_id=1, replica_groups=mesh['tm'=32,'region'=8] {'tm','region'}, use_global_device_ids=true, to_apply=%region_4.5 | all-reduce | flops 2 | bytes 16 | tf_op jit(solution)/shard_map/psum | solution.py:107
  317.6 4.0 fusion.12
  325.8 22.6 %reduce-scatter.7.cloned.1.call-done = f32[1,64,128]{2,1,0:T(8,128)} async-done(((f32[8,64,128]{2,1,0:T(8,128)}), f32[1,64,128]{2,1,0:T(8,128)}) %reduce-scatter.7.cloned.1.call-update) | async-done | bytes 32784 | tf_op jit(solution)/shard_map/reduce_scatter | solution.py:87
  357.8 16.1 %all-gather.3 = f32[512,1,128]{2,1,0:T(1,128)S(1)} all-gather(f32[64,1,128]{2,1,0:T(1,128)S(1)} %bitcast.383), channel_id=5, replica_groups=mesh['tm'=32,'region'=8] {'region'}, dimensions={0}, use_global_device_ids=true | all-gather | bytes 294912 | tf_op jit(solution)/shard_map/all_gather | solution.py:114
  373.9 7.9 fusion.20
  387.2 10.5 %fusion.2 = f32[25,64,3,128]{3,1,2,0:T(8,128)} fusion(f32[1,25,3,128,128]{4,3,2,1,0:T(8,128)} %param.57, f32[64,25,128]{2,0,1:T(8,128)S(1)} %get-tuple-element.275), kind=kOutput, calls=%fused_computation.6 | convolution fusion | flops 943718400 | bytes 8192000 | tf_op jit(solution)/shard_map/hil,iskl->hisk/dot_general | solution.py:29
  397.9 59.1 %psum.76 = f32[128]{0:T(128)S(1)} all-reduce(f32[128]{0:T(128)S(1)} %fusion.47), channel_id=1, replica_groups=mesh['tm'=32,'region'=8] {'tm'}, use_global_device_ids=true, to_apply=%region_20.22 | all-reduce | flops 128 | bytes 1024 | tf_op jit(solution)/shard_map/psum | solution.py:98
  457.0 86.0 %all-reduce.4 = (f32[]{:T(128)}, f32[]{:T(128)}) all-reduce(f32[]{:T(128)S(6)} %add.257, f32[]{:T(128)} %get-tuple-element.274), channel_id=1, replica_groups=mesh['tm'=32,'region'=8] {'tm','region'}, use_global_device_ids=true, to_apply=%region_13.15 | all-reduce | flops 2 | bytes 16 | tf_op jit(solution)/shard_map/psum | solution.py:107
  547.2 4.0 fusion.10
  555.4 23.9 %reduce-scatter.9.cloned.1.call-done = f32[1,64,128]{2,1,0:T(8,128)} async-done(((f32[8,64,128]{2,1,0:T(8,128)}), f32[1,64,128]{2,1,0:T(8,128)}) %reduce-scatter.9.cloned.1.call-update) | async-done | bytes 32784 | tf_op jit(solution)/shard_map/reduce_scatter | solution.py:87
  587.9 16.1 %all-gather.4 = f32[512,1,128]{2,1,0:T(1,128)S(1)} all-gather(f32[64,1,128]{2,1,0:T(1,128)S(1)} %bitcast.384), channel_id=6, replica_groups=mesh['tm'=32,'region'=8] {'region'}, dimensions={0}, use_global_device_ids=true | all-gather | bytes 294912 | tf_op jit(solution)/shard_map/all_gather | solution.py:114
  604.0 7.9 fusion.18
  618.5 10.5 %fusion = f32[25,64,3,128]{3,1,2,0:T(8,128)} fusion(f32[1,25,3,128,128]{4,3,2,1,0:T(8,128)} %param.57, f32[64,25,128]{2,0,1:T(8,128)S(1)} %get-tuple-element.271), kind=kOutput, calls=%fused_computation.4 | convolution fusion | flops 943718400 | bytes 8192000 | tf_op jit(solution)/shard_map/hil,iskl->hisk/dot_general | solution.py:29
  629.2 59.1 %psum.79 = f32[128]{0:T(128)S(1)} all-reduce(f32[128]{0:T(128)S(1)} %fusion.45), channel_id=1, replica_groups=mesh['tm'=32,'region'=8] {'tm'}, use_global_device_ids=true, to_apply=%region_29.31 | all-reduce | flops 128 | bytes 1024 | tf_op jit(solution)/shard_map/psum | solution.py:98
  688.3 86.0 %all-reduce.3 = (f32[]{:T(128)}, f32[]{:T(128)}) all-reduce(f32[]{:T(128)S(6)} %add.266, f32[]{:T(128)} %get-tuple-element.270), channel_id=1, replica_groups=mesh['tm'=32,'region'=8] {'tm','region'}, use_global_device_ids=true, to_apply=%region_22.24 | all-reduce | flops 2 | bytes 16 | tf_op jit(solution)/shard_map/psum | solution.py:107
  786.6 24.2 %reduce-scatter.11.cloned.1.call-done = f32[1,64,128]{2,1,0:T(8,128)} async-done(((f32[8,64,128]{2,1,0:T(8,128)}), f32[1,64,128]{2,1,0:T(8,128)}) %reduce-scatter.11.cloned.1.call-update) | async-done | bytes 32784 | tf_op jit(solution)/shard_map/reduce_scatter | solution.py:87
  819.9 16.1 %all-gather.5 = f32[512,1,128]{2,1,0:T(1,128)S(1)} all-gather(f32[64,1,128]{2,1,0:T(1,128)S(1)} %bitcast.382), channel_id=7, replica_groups=mesh['tm'=32,'region'=8] {'region'}, dimensions={0}, use_global_device_ids=true | all-gather | bytes 294912 | tf_op jit(solution)/shard_map/all_gather | solution.py:114
  836.0 8.0 fusion.16
  (182 shorter events, 94.8 us)
Async XLA Ops:
  7.2 97.1 %copy-start = (f32[64,1,3200]{2,1,0:T(1,128)S(1)}, f32[64,1,3200]{2,1,0:T(1,128)}, u32[]{:S(2)}) copy-start(f32[64,1,3200]{2,1,0:T(1,128)} %param.53) | copy-start | bytes 2457604
  7.2 102.9 %reduce-scatter.5.cloned.1.call-start = ((), (), s32[]{:S(2)}) async-start(), calls=%async_computation.4 | async-start | bytes 294912 | tf_op jit(solution)/shard_map/reduce_scatter | solution.py:87
  7.2 102.8 %collective-permute-start = (f32[128]{0:T(128)S(1)}, f32[128]{0:T(128)S(1)}, u32[]{:S(2)}, u32[]{:S(2)}) collective-permute-start(f32[128]{0:T(128)S(1)} %broadcast.305), channel_id=1, source_target_pairs={{8,0},{16,8},{24,16},{32,24},{40,32},{48,40},{56,48},{64,56},{72,6... | collective-permute-start | bytes 1544 | tf_op jit(solution)/shard_map/ppermute | solution.py:16
  12.0 336.4 %reduce-scatter.7.cloned.1.call-start = ((), (), s32[]{:S(2)}) async-start(), calls=%async_computation.5 | async-start | bytes 294912 | tf_op jit(solution)/shard_map/reduce_scatter | solution.py:87
  24.4 2.6 copy-start.13
  24.4 79.8 %copy-start.11 = (f32[1,3200]{1,0:T(1,128)S(1)}, f32[1,3200]{1,0:T(1,128)}, u32[]{:S(2)}) copy-start(f32[1,3200]{1,0:T(1,128)} %param.54) | copy-start | bytes 38404
  112.0 43.3 %collective-permute-start.1 = (f32[128]{0:T(128)S(1)}, f32[128]{0:T(128)S(1)}, u32[]{:S(2)}, u32[]{:S(2)}) collective-permute-start(f32[128]{0:T(128)S(1)} %slice_bitcast_fusion.16), channel_id=1, source_target_pairs={{0,8},{8,16},{16,24},{24,32},{32,40},{40,48},{48,56},{56,64},{64,7... | collective-permute-start | bytes 1544 | tf_op jit(solution)/shard_map/ppermute | solution.py:16
  151.5 3.8 copy-start.2
  156.6 10.9 %copy-start.8 = (f32[64,25,128]{2,0,1:T(8,128)}, f32[64,25,128]{2,0,1:T(8,128)S(1)}, u32[]{:S(2)}) copy-start(f32[64,25,128]{2,0,1:T(8,128)S(1)} %get-tuple-element.281) | copy-start | bytes 2457604
  167.7 153.9 %copy-start.15 = (s32[1,128]{1,0:T(1,128)S(1)}, s32[1,128]{1,0:T(1,128)}, u32[]{:S(2)}) copy-start(s32[1,128]{1,0:T(1,128)} %param.61) | copy-start | bytes 1540
  314.6 10.5 %collective-permute-start.2 = (f32[128]{0:T(128)S(1)}, f32[128]{0:T(128)S(1)}, u32[]{:S(2)}, u32[]{:S(2)}) collective-permute-start(f32[128]{0:T(128)S(1)} %slice_bitcast_fusion.15), channel_id=1, source_target_pairs={{8,0},{16,8},{24,16},{32,24},{40,32},{48,40},{56,48},{64,56},{72,6... | collective-permute-start | bytes 1544 | tf_op jit(solution)/shard_map/ppermute | solution.py:16
  317.1 262.2 %reduce-scatter.9.cloned.1.call-start = ((), (), s32[]{:S(2)}) async-start(), calls=%async_computation.6 | async-start | bytes 294912 | tf_op jit(solution)/shard_map/reduce_scatter | solution.py:87
  354.9 30.4 %collective-permute-start.3 = (f32[128]{0:T(128)S(1)}, f32[128]{0:T(128)S(1)}, u32[]{:S(2)}, u32[]{:S(2)}) collective-permute-start(f32[128]{0:T(128)S(1)} %slice_bitcast_fusion.14), channel_id=1, source_target_pairs={{0,8},{8,16},{16,24},{24,32},{32,40},{40,48},{48,56},{56,64},{64,7... | collective-permute-start | bytes 1544 | tf_op jit(solution)/shard_map/ppermute | solution.py:16
  381.8 4.0 copy-start.9
  386.8 10.9 %copy-start.7 = (f32[64,25,128]{2,0,1:T(8,128)}, f32[64,25,128]{2,0,1:T(8,128)S(1)}, u32[]{:S(2)}) copy-start(f32[64,25,128]{2,0,1:T(8,128)S(1)} %get-tuple-element.275) | copy-start | bytes 2457604
  544.5 10.3 %collective-permute-start.4 = (f32[128]{0:T(128)S(1)}, f32[128]{0:T(128)S(1)}, u32[]{:S(2)}, u32[]{:S(2)}) collective-permute-start(f32[128]{0:T(128)S(1)} %slice_bitcast_fusion.13), channel_id=1, source_target_pairs={{8,0},{16,8},{24,16},{32,24},{40,32},{48,40},{56,48},{64,56},{72,6... | collective-permute-start | bytes 1544 | tf_op jit(solution)/shard_map/ppermute | solution.py:16
  547.0 263.9 %reduce-scatter.11.cloned.1.call-start = ((), (), s32[]{:S(2)}) async-start(), calls=%async_computation.7 | async-start | bytes 294912 | tf_op jit(solution)/shard_map/reduce_scatter | solution.py:87
  551.2 29.5 %copy-start.4 = (f32[64,25,128]{2,0,1:T(8,128)S(1)}, f32[64,25,128]{2,0,1:T(8,128)}, u32[]{:S(2)}) copy-start(f32[64,25,128]{2,0,1:T(8,128)} %copy-done.3) | copy-start | bytes 2457604
  585.1 30.5 %collective-permute-start.5 = (f32[128]{0:T(128)S(1)}, f32[128]{0:T(128)S(1)}, u32[]{:S(2)}, u32[]{:S(2)}) collective-permute-start(f32[128]{0:T(128)S(1)} %slice_bitcast_fusion.12), channel_id=1, source_target_pairs={{0,8},{8,16},{16,24},{24,32},{32,40},{40,48},{48,56},{56,64},{64,7... | collective-permute-start | bytes 1544 | tf_op jit(solution)/shard_map/ppermute | solution.py:16
  618.1 10.9 %copy-start.5 = (f32[64,25,128]{2,0,1:T(8,128)}, f32[64,25,128]{2,0,1:T(8,128)S(1)}, u32[]{:S(2)}) copy-start(f32[64,25,128]{2,0,1:T(8,128)S(1)} %get-tuple-element.271) | copy-start | bytes 2457604
  775.8 10.2 %collective-permute-start.6 = (f32[128]{0:T(128)S(1)}, f32[128]{0:T(128)S(1)}, u32[]{:S(2)}, u32[]{:S(2)}) collective-permute-start(f32[128]{0:T(128)S(1)} %slice_bitcast_fusion.11), channel_id=1, source_target_pairs={{8,0},{16,8},{24,16},{32,24},{40,32},{48,40},{56,48},{64,56},{72,6... | collective-permute-start | bytes 1544 | tf_op jit(solution)/shard_map/ppermute | solution.py:16
  817.0 31.6 %collective-permute-start.7 = (f32[128]{0:T(128)S(1)}, f32[128]{0:T(128)S(1)}, u32[]{:S(2)}, u32[]{:S(2)}) collective-permute-start(f32[128]{0:T(128)S(1)} %slice_bitcast_fusion.10), channel_id=1, source_target_pairs={{0,8},{8,16},{16,24},{24,32},{32,40},{40,48},{48,56},{56,64},{64,7... | collective-permute-start | bytes 1544 | tf_op jit(solution)/shard_map/ppermute | solution.py:16
  836.0 8.4 copy-start.10
  844.9 4.1 copy-start.6
  (5 other events, 8.1 us)
Sparse Core Ops, SparseCore 0:
  12.1 36.2 reduce-scatter.4
  317.2 31.0 reduce-scatter.6
  547.1 32.1 reduce-scatter.8
  778.6 32.1 reduce-scatter.10
where the time goes:
time: 867 us; the launch traced here: 858 us
  blocking collectives  589 us (68%)
  matrix products  94.9 us (11%)
  waiting for transfers between devices  70.8 us (8%)
  other arithmetic  35 us (4%)
  local copies, waits for them, and re-layouts  28.8 us (3%)
  between operations  23.7 us (3%)
  starting transfers between devices  16 us (2%)
    psum x3, blocking collectives, body(): primal_total = lax.psum(primal_local, ('tm', 'region'))  262 us
    psum x3, blocking collectives, body(): capacity_grad = lax.psum(capacity_part, 'tm')  174 us
    all_gather x1, blocking collectives, body(): lax.all_gather(start_capacity[0], 'tm', axis=0, tiled=True)  76.9 us
    all_gather x4, blocking collectives, body(): lax.all_gather(primal_bar[:, 3][None], 'region', axis=0, tiled=True)  76.5 us
    reduce_scatter x4, waiting for transfers between devices, body(): lax.psum_scatter(jnp.einsum('jq,jhk->qhk', own_sources, partial_lines, pr...  70.7 us
    dot_general x4, matrix products, network_adjoint(): jnp.einsum('hil,iskl->hisk', dual_rows, weights, precision=HIGHEST_PRECIS...  40.4 us
    dot_general x4, matrix products, network_forward(): jnp.einsum('hpk,pkl->hpl', picked, flat_weights, precision=HIGHEST_PRECIS...  31.7 us
  transfers between devices with their start and end apart: 12, of which 3 were waited for; matrix products, arithmetic and copies ran while one was open for 11% of the time, Pallas kernels for 0%

commit v1 on v0

--- a/solution.py
+++ b/solution.py
@@ -104,7 +104,11 @@
         primal_bar = 2.0 * new_primal - primal
         primal_local = jnp.sum((new_primal - primal) ** 2) + jnp.sum(capacity_change**2)
         if iteration + 1 < ITERS:
-            primal_total = lax.psum(primal_local, ("tm", "region"))
+
+            def feed_unit_for(dev_axis, local_x, row_axis):
+                return jax.lax.psum(jax.lax.psum(local_x, dev_axis), row_axis)
+
+            primal_total = feed_unit_for("tm", primal_local, "region")
         applied = network_forward(primal_bar, weights, columns)
         before = shifted(primal_bar[-1, 0], "tm", 1)
         earlier = jnp.concatenate([before[None], primal_bar[:-1, 0]], axis=0)

time: 867 us -> 904 us (1.043)
  blocking collectives: 589 us -> 638 us
  waiting for transfers between devices: 70.8 us -> 59 us
    psum x6 -> x9, blocking collectives: 436 us -> 484 us  [the longest x6 257 us: feed_unit_for(): return jax.lax.psum(jax.lax.psum(local_x, dev_axis), row_axis)]
    reduce_scatter x4, waiting for transfers between devices: 70.7 us -> 58.9 us  [body(): lax.psum_scatter(jnp.einsum('jq,jhk->qhk', own_sources, partial_lines, pr...]
where the time goes in v1:
time: 904 us; the launch traced here: 895 us
  blocking collectives  638 us (71%)
  matrix products  94.9 us (10%)
  waiting for transfers between devices  59 us (7%)
  other arithmetic  35 us (4%)
  local copies, waits for them, and re-layouts  28.8 us (3%)
  between operations  23.8 us (3%)
  starting transfers between devices  16 us (2%)
    psum x6, blocking collectives, feed_unit_for(): return jax.lax.psum(jax.lax.psum(local_x, dev_axis), row_axis)  257 us
    psum x3, blocking collectives, body(): dual_total = lax.psum(dual_local, ('tm', 'region'))  228 us
    all_gather x1, blocking collectives, body(): lax.all_gather(start_capacity[0], 'tm', axis=0, tiled=True)  76.9 us
    all_gather x4, blocking collectives, body(): lax.all_gather(primal_bar[:, 3][None], 'region', axis=0, tiled=True)  76.4 us
    reduce_scatter x4, waiting for transfers between devices, body(): lax.psum_scatter(jnp.einsum('jq,jhk->qhk', own_sources, partial_lines, pr...  58.9 us
    dot_general x4, matrix products, network_adjoint(): jnp.einsum('hil,iskl->hisk', dual_rows, weights, precision=HIGHEST_PRECIS...  40.4 us
    dot_general x4, matrix products, network_forward(): jnp.einsum('hpk,pkl->hpl', picked, flat_weights, precision=HIGHEST_PRECIS...  31.7 us
  transfers between devices with their start and end apart: 12, of which 3 were waited for; matrix products, arithmetic and copies ran while one was open for 11% of the time, Pallas kernels for 0%

profile of v1, /device:TPU:1, one launch (start us, length us, event | category | flops | bytes accessed | tf_op | source)
XLA Modules:
  0.0 895.2 jit_solution(10128880783119224581)
XLA Ops:
  12.9 9.0 %fusion.6 = f32[25,64,3,128]{3,1,2,0:T(8,128)S(1)} fusion(f32[1,25,3,128,128]{4,3,2,1,0:T(8,128)} %param.57), kind=kOutput, calls=%fused_computation.10 | convolution fusion | flops 943718400 | bytes 7372800 | tf_op jit(solution)/shard_map/hil,iskl->hisk/dot_general | solution.py:29
  27.1 76.9 %all-reduce.6 = (f32[128]{0:T(128)S(1)}, f32[128]{0:T(128)S(1)}, f32[128]{0:T(128)S(1)}) all-reduce(f32[128]{0:T(128)S(1)} %bitcast_dynamic-update-slice_fusion.1, f32[128]{0:T(128)S(1)} %bitcast_dynamic-update-slice_fusion, f32[128]{0:T(128)S(1)} %fusion.51), channel_id=2, replica_groups=mesh['tm'=32,'region'=8] {'tm'}, use_global_device_ids=true, to_apply=%add.1 | all-reduce | flops 384 | bytes 3072 | tf_op jit(solution)/shard_map/all_gather | solution.py:75
  113.4 28.2 %all-gather.2 = f32[512,1,128]{2,1,0:T(1,128)S(1)} all-gather(f32[64,1,128]{2,1,0:T(1,128)S(1)} %bitcast.385), channel_id=4, replica_groups=mesh['tm'=32,'region'=8] {'region'}, dimensions={0}, use_global_device_ids=true | all-gather | bytes 294912 | tf_op jit(solution)/shard_map/all_gather | solution.py:118
  143.7 7.9 fusion.22
  157.1 10.5 %fusion.4 = f32[25,64,3,128]{3,1,2,0:T(8,128)} fusion(f32[1,25,3,128,128]{4,3,2,1,0:T(8,128)} %param.57, f32[64,25,128]{2,0,1:T(8,128)S(1)} %get-tuple-element.281), kind=kOutput, calls=%fused_computation.8 | convolution fusion | flops 943718400 | bytes 8192000 | tf_op jit(solution)/shard_map/hil,iskl->hisk/dot_general | solution.py:29
  167.6 75.8 %psum.94 = f32[]{:T(128)} all-reduce(f32[]{:T(128)} %get-tuple-element.280), channel_id=1, replica_groups=mesh['tm'=32,'region'=8] {'tm','region'}, use_global_device_ids=true, to_apply=%region_8.10 | all-reduce | flops 1 | bytes 8 | tf_op jit(solution)/shard_map/psum | solution.py:135
  244.3 57.9 %all-reduce.5 = (f32[]{:T(128)}, f32[128]{0:T(128)S(1)}) all-reduce(f32[]{:T(128)S(6)} %add.255, f32[128]{0:T(128)S(1)} %fusion.49), channel_id=1, replica_groups=mesh['tm'=32,'region'=8] {'tm'}, use_global_device_ids=true, to_apply=%region_4.5 | all-reduce | flops 129 | bytes 1032 | tf_op jit(solution)/shard_map/psum | solution.py:109
  302.2 26.7 %psum.93 = f32[]{:T(128)} all-reduce(f32[]{:T(128)} %get-tuple-element.263), channel_id=1, replica_groups=mesh['tm'=32,'region'=8] {'region'}, use_global_device_ids=true, to_apply=%region_5.6 | all-reduce | flops 1 | bytes 8 | tf_op jit(solution)/shard_map/psum | solution.py:109
  340.9 19.9 %reduce-scatter.7.cloned.1.call-done = f32[1,64,128]{2,1,0:T(8,128)} async-done(((f32[8,64,128]{2,1,0:T(8,128)}), f32[1,64,128]{2,1,0:T(8,128)}) %reduce-scatter.7.cloned.1.call-update) | async-done | bytes 32784 | tf_op jit(solution)/shard_map/reduce_scatter | solution.py:87
  370.2 16.1 %all-gather.3 = f32[512,1,128]{2,1,0:T(1,128)S(1)} all-gather(f32[64,1,128]{2,1,0:T(1,128)S(1)} %bitcast.383), channel_id=5, replica_groups=mesh['tm'=32,'region'=8] {'region'}, dimensions={0}, use_global_device_ids=true | all-gather | bytes 294912 | tf_op jit(solution)/shard_map/all_gather | solution.py:118
  386.3 7.9 fusion.20
  399.6 10.5 %fusion.2 = f32[25,64,3,128]{3,1,2,0:T(8,128)} fusion(f32[1,25,3,128,128]{4,3,2,1,0:T(8,128)} %param.57, f32[64,25,128]{2,0,1:T(8,128)S(1)} %get-tuple-element.275), kind=kOutput, calls=%fused_computation.6 | convolution fusion | flops 943718400 | bytes 8192000 | tf_op jit(solution)/shard_map/hil,iskl->hisk/dot_general | solution.py:29
  410.1 76.0 %psum.98 = f32[]{:T(128)} all-reduce(f32[]{:T(128)} %get-tuple-element.274), channel_id=1, replica_groups=mesh['tm'=32,'region'=8] {'tm','region'}, use_global_device_ids=true, to_apply=%region_18.20 | all-reduce | flops 1 | bytes 8 | tf_op jit(solution)/shard_map/psum | solution.py:135
  487.1 58.7 %all-reduce.4 = (f32[]{:T(128)}, f32[128]{0:T(128)S(1)}) all-reduce(f32[]{:T(128)S(6)} %add.263, f32[128]{0:T(128)S(1)} %fusion.47), channel_id=1, replica_groups=mesh['tm'=32,'region'=8] {'tm'}, use_global_device_ids=true, to_apply=%region_14.16 | all-reduce | flops 129 | bytes 1032 | tf_op jit(solution)/shard_map/psum | solution.py:109
  545.8 27.2 %psum.97 = f32[]{:T(128)} all-reduce(f32[]{:T(128)} %get-tuple-element.261), channel_id=1, replica_groups=mesh['tm'=32,'region'=8] {'region'}, use_global_device_ids=true, to_apply=%region_15.17 | all-reduce | flops 1 | bytes 8 | tf_op jit(solution)/shard_map/psum | solution.py:109
  584.7 19.3 %reduce-scatter.9.cloned.1.call-done = f32[1,64,128]{2,1,0:T(8,128)} async-done(((f32[8,64,128]{2,1,0:T(8,128)}), f32[1,64,128]{2,1,0:T(8,128)}) %reduce-scatter.9.cloned.1.call-update) | async-done | bytes 32784 | tf_op jit(solution)/shard_map/reduce_scatter | solution.py:87
  612.6 16.1 %all-gather.4 = f32[512,1,128]{2,1,0:T(1,128)S(1)} all-gather(f32[64,1,128]{2,1,0:T(1,128)S(1)} %bitcast.384), channel_id=6, replica_groups=mesh['tm'=32,'region'=8] {'region'}, dimensions={0}, use_global_device_ids=true | all-gather | bytes 294912 | tf_op jit(solution)/shard_map/all_gather | solution.py:118
  643.3 10.5 %fusion = f32[25,64,3,128]{3,1,2,0:T(8,128)} fusion(f32[1,25,3,128,128]{4,3,2,1,0:T(8,128)} %param.57, f32[64,25,128]{2,0,1:T(8,128)S(1)} %get-tuple-element.271), kind=kOutput, calls=%fused_computation.4 | convolution fusion | flops 943718400 | bytes 8192000 | tf_op jit(solution)/shard_map/hil,iskl->hisk/dot_general | solution.py:29
  653.7 76.0 %psum.102 = f32[]{:T(128)} all-reduce(f32[]{:T(128)} %get-tuple-element.270), channel_id=1, replica_groups=mesh['tm'=32,'region'=8] {'tm','region'}, use_global_device_ids=true, to_apply=%region_28.30 | all-reduce | flops 1 | bytes 8 | tf_op jit(solution)/shard_map/psum | solution.py:135
  730.7 58.7 %all-reduce.3 = (f32[]{:T(128)}, f32[128]{0:T(128)S(1)}) all-reduce(f32[]{:T(128)S(6)} %add.272, f32[128]{0:T(128)S(1)} %fusion.45), channel_id=1, replica_groups=mesh['tm'=32,'region'=8] {'tm'}, use_global_device_ids=true, to_apply=%region_24.26 | all-reduce | flops 129 | bytes 1032 | tf_op jit(solution)/shard_map/psum | solution.py:109
  789.3 27.2 %psum.101 = f32[]{:T(128)} all-reduce(f32[]{:T(128)} %get-tuple-element.259), channel_id=1, replica_groups=mesh['tm'=32,'region'=8] {'region'}, use_global_device_ids=true, to_apply=%region_25.27 | all-reduce | flops 1 | bytes 8 | tf_op jit(solution)/shard_map/psum | solution.py:109
  828.2 19.6 %reduce-scatter.11.cloned.1.call-done = f32[1,64,128]{2,1,0:T(8,128)} async-done(((f32[8,64,128]{2,1,0:T(8,128)}), f32[1,64,128]{2,1,0:T(8,128)}) %reduce-scatter.11.cloned.1.call-update) | async-done | bytes 32784 | tf_op jit(solution)/shard_map/reduce_scatter | solution.py:87
  856.8 16.1 %all-gather.5 = f32[512,1,128]{2,1,0:T(1,128)S(1)} all-gather(f32[64,1,128]{2,1,0:T(1,128)S(1)} %bitcast.382), channel_id=7, replica_groups=mesh['tm'=32,'region'=8] {'region'}, dimensions={0}, use_global_device_ids=true | all-gather | bytes 294912 | tf_op jit(solution)/shard_map/all_gather | solution.py:118
  872.9 8.0 fusion.16
  (185 shorter events, 110.7 us)
Async XLA Ops:
  7.2 97.2 %copy-start = (f32[64,1,3200]{2,1,0:T(1,128)S(1)}, f32[64,1,3200]{2,1,0:T(1,128)}, u32[]{:S(2)}) copy-start(f32[64,1,3200]{2,1,0:T(1,128)} %param.53) | copy-start | bytes 2457604
  7.2 103.0 %reduce-scatter.5.cloned.1.call-start = ((), (), s32[]{:S(2)}) async-start(), calls=%async_computation.4 | async-start | bytes 294912 | tf_op jit(solution)/shard_map/reduce_scatter | solution.py:87
  7.2 102.9 %collective-permute-start = (f32[128]{0:T(128)S(1)}, f32[128]{0:T(128)S(1)}, u32[]{:S(2)}, u32[]{:S(2)}) collective-permute-start(f32[128]{0:T(128)S(1)} %broadcast.305), channel_id=1, source_target_pairs={{8,0},{16,8},{24,16},{32,24},{40,32},{48,40},{56,48},{64,56},{72,6... | collective-permute-start | bytes 1544 | tf_op jit(solution)/shard_map/ppermute | solution.py:16
  12.0 348.8 %reduce-scatter.7.cloned.1.call-start = ((), (), s32[]{:S(2)}) async-start(), calls=%async_computation.5 | async-start | bytes 294912 | tf_op jit(solution)/shard_map/reduce_scatter | solution.py:87
  24.4 2.6 copy-start.13
  24.4 79.8 %copy-start.11 = (f32[1,3200]{1,0:T(1,128)S(1)}, f32[1,3200]{1,0:T(1,128)}, u32[]{:S(2)}) copy-start(f32[1,3200]{1,0:T(1,128)} %param.54) | copy-start | bytes 38404
  112.1 43.3 %collective-permute-start.1 = (f32[128]{0:T(128)S(1)}, f32[128]{0:T(128)S(1)}, u32[]{:S(2)}, u32[]{:S(2)}) collective-permute-start(f32[128]{0:T(128)S(1)} %slice_bitcast_fusion.16), channel_id=1, source_target_pairs={{0,8},{8,16},{16,24},{24,32},{32,40},{40,48},{48,56},{56,64},{64,7... | collective-permute-start | bytes 1544 | tf_op jit(solution)/shard_map/ppermute | solution.py:16
  151.6 3.8 copy-start.2
  156.7 10.9 %copy-start.8 = (f32[64,25,128]{2,0,1:T(8,128)}, f32[64,25,128]{2,0,1:T(8,128)S(1)}, u32[]{:S(2)}) copy-start(f32[64,25,128]{2,0,1:T(8,128)S(1)} %get-tuple-element.281) | copy-start | bytes 2457604
  243.6 93.2 %copy-start.15 = (s32[1,128]{1,0:T(1,128)S(1)}, s32[1,128]{1,0:T(1,128)}, u32[]{:S(2)}) copy-start(s32[1,128]{1,0:T(1,128)} %param.61) | copy-start | bytes 1540
  329.7 10.5 %collective-permute-start.2 = (f32[128]{0:T(128)S(1)}, f32[128]{0:T(128)S(1)}, u32[]{:S(2)}, u32[]{:S(2)}) collective-permute-start(f32[128]{0:T(128)S(1)} %slice_bitcast_fusion.15), channel_id=1, source_target_pairs={{8,0},{16,8},{24,16},{32,24},{40,32},{48,40},{56,48},{64,56},{72,6... | collective-permute-start | bytes 1544 | tf_op jit(solution)/shard_map/ppermute | solution.py:16
  332.2 271.9 %reduce-scatter.9.cloned.1.call-start = ((), (), s32[]{:S(2)}) async-start(), calls=%async_computation.6 | async-start | bytes 294912 | tf_op jit(solution)/shard_map/reduce_scatter | solution.py:87
  367.4 30.5 %collective-permute-start.3 = (f32[128]{0:T(128)S(1)}, f32[128]{0:T(128)S(1)}, u32[]{:S(2)}, u32[]{:S(2)}) collective-permute-start(f32[128]{0:T(128)S(1)} %slice_bitcast_fusion.14), channel_id=1, source_target_pairs={{0,8},{8,16},{16,24},{24,32},{32,40},{40,48},{48,56},{56,64},{64,7... | collective-permute-start | bytes 1544 | tf_op jit(solution)/shard_map/ppermute | solution.py:16
  394.2 4.0 copy-start.9
  399.2 10.9 %copy-start.7 = (f32[64,25,128]{2,0,1:T(8,128)}, f32[64,25,128]{2,0,1:T(8,128)S(1)}, u32[]{:S(2)}) copy-start(f32[64,25,128]{2,0,1:T(8,128)S(1)} %get-tuple-element.275) | copy-start | bytes 2457604
  573.8 10.3 %collective-permute-start.4 = (f32[128]{0:T(128)S(1)}, f32[128]{0:T(128)S(1)}, u32[]{:S(2)}, u32[]{:S(2)}) collective-permute-start(f32[128]{0:T(128)S(1)} %slice_bitcast_fusion.13), channel_id=1, source_target_pairs={{8,0},{16,8},{24,16},{32,24},{40,32},{48,40},{56,48},{64,56},{72,6... | collective-permute-start | bytes 1544 | tf_op jit(solution)/shard_map/ppermute | solution.py:16
  576.3 271.5 %reduce-scatter.11.cloned.1.call-start = ((), (), s32[]{:S(2)}) async-start(), calls=%async_computation.7 | async-start | bytes 294912 | tf_op jit(solution)/shard_map/reduce_scatter | solution.py:87
  580.5 24.9 %copy-start.4 = (f32[64,25,128]{2,0,1:T(8,128)S(1)}, f32[64,25,128]{2,0,1:T(8,128)}, u32[]{:S(2)}) copy-start(f32[64,25,128]{2,0,1:T(8,128)} %copy-done.3) | copy-start | bytes 2457604
  609.8 30.5 %collective-permute-start.5 = (f32[128]{0:T(128)S(1)}, f32[128]{0:T(128)S(1)}, u32[]{:S(2)}, u32[]{:S(2)}) collective-permute-start(f32[128]{0:T(128)S(1)} %slice_bitcast_fusion.12), channel_id=1, source_target_pairs={{0,8},{8,16},{16,24},{24,32},{32,40},{40,48},{48,56},{56,64},{64,7... | collective-permute-start | bytes 1544 | tf_op jit(solution)/shard_map/ppermute | solution.py:16
  642.8 10.9 %copy-start.5 = (f32[64,25,128]{2,0,1:T(8,128)}, f32[64,25,128]{2,0,1:T(8,128)S(1)}, u32[]{:S(2)}) copy-start(f32[64,25,128]{2,0,1:T(8,128)S(1)} %get-tuple-element.271) | copy-start | bytes 2457604
  817.4 10.2 %collective-permute-start.6 = (f32[128]{0:T(128)S(1)}, f32[128]{0:T(128)S(1)}, u32[]{:S(2)}, u32[]{:S(2)}) collective-permute-start(f32[128]{0:T(128)S(1)} %slice_bitcast_fusion.11), channel_id=1, source_target_pairs={{8,0},{16,8},{24,16},{32,24},{40,32},{48,40},{56,48},{64,56},{72,6... | collective-permute-start | bytes 1544 | tf_op jit(solution)/shard_map/ppermute | solution.py:16
  854.0 31.6 %collective-permute-start.7 = (f32[128]{0:T(128)S(1)}, f32[128]{0:T(128)S(1)}, u32[]{:S(2)}, u32[]{:S(2)}) collective-permute-start(f32[128]{0:T(128)S(1)} %slice_bitcast_fusion.10), channel_id=1, source_target_pairs={{0,8},{8,16},{16,24},{24,32},{32,40},{40,48},{48,56},{56,64},{64,7... | collective-permute-start | bytes 1544 | tf_op jit(solution)/shard_map/ppermute | solution.py:16
  872.9 8.4 copy-start.10
  881.8 4.1 copy-start.6
  (5 other events, 8.1 us)
Sparse Core Ops, SparseCore 0:
  12.1 36.2 reduce-scatter.4
  332.3 28.4 reduce-scatter.6
  576.4 27.6 reduce-scatter.8
  820.2 27.5 reduce-scatter.10
